TPU v7x, 512 devices: a whole 4x8x8 slice. The times are simulated.
512 devices in a mesh: row: 16 (over y, core), col: 32 (over z, x).
Axes of the slice: x: 4, y: 8, z: 8, core: 2. Of those that a mesh axis runs over, the one named last changes fastest.
Arguments:
- surface: float32 [2, 1024, 4096], P(None, 'row', 'col'), may hold values from -0.5 to 0.5
- u_face: float32 [2, 1024, 4096], P(None, 'row', 'col'), may hold values from -3 to 3
- v_face: float32 [2, 1024, 4096], P(None, 'row', 'col'), may hold values from -3 to 3
- bed_depth: float32 [1024, 4096], P('row', 'col'), may hold values from 1 to 10
- wet_mask: int32 [2, 1024, 4096], P(None, 'row', 'col'), may hold values 0 or 1
- rainfall: float32 [2, 1024, 4096], P(None, 'row', 'col'), may hold values from 0.05 to 0.5
Outputs:
- new_surface: float32 [2, 1024, 4096], P(None, 'row', 'col')
- new_u: float32 [2, 1024, 4096], P(None, 'row', 'col')
- new_v: float32 [2, 1024, 4096], P(None, 'row', 'col')
All inputs are finite; a program needn't handle non-finite values. No bound on the sum of `wet_mask` on one device may be relied on, other than what follows from the above.
Results may differ from a plain program's by a relative error of at most 0.0003.
Values sent between devices are 32-bit elements; how exact they have to be, the bound alone decides.
A program may use at most 64 MiB of HBM per device.

v0:
```python
import jax
import jax.numpy as jnp
from jax import lax
from jax.sharding import PartitionSpec as P

ITERS = 3


DTDX = 0.5
FRIC = 0.05
G1 = 4.0
CK = DTDX * G1


def extended(cells, sides, width):
    for axis, dim in sides:
        count = lax.axis_size(axis)
        ends = count - 1
        head = lax.slice_in_dim(cells, 0, width, axis=dim)
        tail = lax.slice_in_dim(cells, cells.shape[dim] - width, cells.shape[dim], axis=dim)
        cells = jnp.concatenate(
            [
                lax.ppermute(tail, axis, [(i, (i + 1) % count) for i in range(ends)]),
                cells,
                lax.ppermute(head, axis, [((i + 1) % count, i) for i in range(ends)]),
            ],
            axis=dim,
        )
    return cells


def passed_along(block, axis, distance):
    devices = range(lax.axis_size(axis))
    route = [(i - distance, i) for i in devices if i - distance in devices]
    return lax.ppermute(block, axis, route)


def explicit(eta2, u2, v2, dep2, wet2, ny, nx):

    def view(a, dy, dx):
        return a[:, 1 + dy : 3 + dy + ny, 1 + dx : 3 + dx + nx]

    h_here = view(eta2, 0, 0) + view(dep2, 0, 0)
    h_east = view(eta2, 0, 1) + view(dep2, 0, 1)
    h_north = view(eta2, 1, 0) + view(dep2, 1, 0)
    wet_x = view(wet2, 0, 0) * view(wet2, 0, 1)
    wet_y = view(wet2, 0, 0) * view(wet2, 1, 0)
    depth_x = 0.5 * (h_here + h_east)
    depth_y = 0.5 * (h_here + h_north)
    u_here = view(u2, 0, 0)
    v_here = view(v2, 0, 0)
    v_mean = 0.25 * (v_here + view(v2, 0, 1) + view(v2, -1, 0) + view(v2, -1, 1))
    u_mean = 0.25 * (u_here + view(u2, 0, -1) + view(u2, 1, 0) + view(u2, 1, -1))
    adv_u = jnp.where(
        u_here > 0, u_here * (u_here - view(u2, 0, -1)), u_here * (view(u2, 0, 1) - u_here)
    )
    adv_u = adv_u + jnp.where(
        v_mean > 0, v_mean * (u_here - view(u2, -1, 0)), v_mean * (view(u2, 1, 0) - u_here)
    )
    adv_v = jnp.where(
        v_here > 0, v_here * (v_here - view(v2, -1, 0)), v_here * (view(v2, 1, 0) - v_here)
    )
    adv_v = adv_v + jnp.where(
        u_mean > 0, u_mean * (v_here - view(v2, 0, -1)), u_mean * (view(v2, 0, 1) - v_here)
    )
    u_star = wet_x * (u_here - DTDX * adv_u) / (1.0 + FRIC * jnp.abs(u_here))
    v_star = wet_y * (v_here - DTDX * adv_v) / (1.0 + FRIC * jnp.abs(v_here))
    return (
        u_star,
        v_star,
        wet_x,
        wet_y,
        CK * depth_x * wet_x,
        CK * depth_y * wet_y,
        depth_x * u_star,
        depth_y * v_star,
    )


def inner(a):
    return a[:, 1:-1, 1:-1]


def right_side(eta, rain, flux_x, flux_y):
    div = inner(flux_x) - flux_x[:, 1:-1, :-2] + (inner(flux_y) - flux_y[:, :-2, 1:-1])
    return eta + rain - DTDX * div


def operate(e_pad, coef_x, coef_y):
    e_mid = inner(e_pad)
    out = (
        e_mid
        + inner(coef_x) * (e_mid - e_pad[:, 1:-1, 2:])
        + coef_x[:, 1:-1, :-2] * (e_mid - e_pad[:, 1:-1, :-2])
    )
    return (
        out
        + inner(coef_y) * (e_mid - e_pad[:, 2:, 1:-1])
        + coef_y[:, :-2, 1:-1] * (e_mid - e_pad[:, :-2, 1:-1])
    )


def field_pad(field):
    return extended(field, (("row", 1), ("col", 2)), 1)


def squares(residual):
    return lax.psum(jnp.sum(residual * residual, axis=(1, 2)), ("row", "col"))


def spread(values):
    return values[:, None, None]


def body(surface, u_face, v_face, bed_depth, wet_mask, rainfall):
    rows = surface.shape[1]
    cols = surface.shape[2]
    stacked = jnp.stack(
        [
            surface,
            u_face,
            v_face,
            jnp.broadcast_to(bed_depth[None], surface.shape),
            wet_mask.astype(jnp.float32),
        ]
    )
    padded = extended(stacked, (("row", 2), ("col", 3)), 2)
    u_star, v_star, wet_x, wet_y, coef_x, coef_y, flux_x, flux_y = explicit(
        padded[0], padded[1], padded[2], padded[3], padded[4], rows, cols
    )
    rhs = right_side(surface, rainfall, flux_x, flux_y)
    start_pad = padded[0][:, 1:-1, 1:-1]
    solution = surface
    residual = rhs - operate(start_pad, coef_x, coef_y)
    direction = residual
    norm_now = squares(residual)
    for step in range(ITERS):
        direction_pad = field_pad(direction)
        image = operate(direction_pad, coef_x, coef_y)
        alpha = norm_now / lax.psum(jnp.sum(direction * image, axis=(1, 2)), ("row", "col"))
        solution = solution + spread(alpha) * direction
        residual = residual - spread(alpha) * image
        norm_next = squares(residual)
        direction = residual + spread(norm_next / norm_now) * direction
        norm_now = norm_next
    east_col = passed_along(solution[:, :, :1], "col", -1)
    north_row = passed_along(solution[:, :1, :], "row", -1)
    east_field = jnp.concatenate([solution[:, :, 1:], east_col], axis=2)
    north_field = jnp.concatenate([solution[:, 1:, :], north_row], axis=1)
    new_u = inner(u_star) - G1 * inner(wet_x) * (east_field - solution)
    new_v = inner(v_star) - G1 * inner(wet_y) * (north_field - solution)
    return (solution, new_u, new_v)


def solution(mesh):
    in_specs = (
        P(None, "row", "col"),
        P(None, "row", "col"),
        P(None, "row", "col"),
        P("row", "col"),
        P(None, "row", "col"),
        P(None, "row", "col"),
    )
    out_specs = (P(None, "row", "col"), P(None, "row", "col"), P(None, "row", "col"))
    return jax.shard_map(body, mesh=mesh, in_specs=in_specs, out_specs=out_specs, check_vma=False)
```

profile of v0, /device:TPU:1, one launch (start us, length us, event | category | flops | bytes accessed | tf_op | source)
XLA Modules:
  0.0 588.9 jit_solution(1745346275453686401)
XLA Ops:
  0.6 0.9 bitcast_dynamic-update-slice_fusion.3
  3.1 0.8 copy-done.5
  4.0 4.6 collective-permute-start
  8.6 5.5 collective-permute-start.1
  15.1 1.8 collective-permute-start.2
  16.9 1.3 collective-permute-start.3
  18.2 7.1 %collective-permute-done.2 = f32[5,2,68,2]{3,2,1,0:T(8,128)S(1)} collective-permute-done((f32[5,2,68,2]{3,2,1,0:T(8,128)S(1)}, f32[5,2,68,2]{3,2,1,0:T(8,128)S(1)}, u32[]{:S(2)}, u32[]{:S(2)}) %collective-permute-start.2) | collective-permute-done | bytes 5472 | tf_op jit(solution)/shard_map/ppermute | solution.py:23
  25.3 3.9 collective-permute-done.3
  31.6 2.6 collective-permute-start.5
  34.2 3.0 collective-permute-start.4
  37.9 1.3 collective-permute-start.6
  39.2 4.0 collective-permute-start.7
  43.2 0.9 collective-permute-done.6
  44.1 0.9 collective-permute-done.7
  45.3 111.8 %all-reduce = (f32[2]{0:T(128)S(1)}, f32[2]{0:T(128)S(1)}) all-reduce(f32[2]{0:T(128)S(1)} %get-tuple-element.4, f32[2]{0:T(128)S(1)} %get-tuple-element.3), channel_id=1, replica_groups=mesh['row'=16,'col'=32] {'row','col'}, use_global_device_ids=true, to_apply=%region_1.2 | all-reduce | flops 4 | bytes 32 | tf_op jit(solution)/shard_map/psum | solution.py:108
  157.3 95.3 %psum.44 = f32[2]{0:T(128)S(1)} all-reduce(f32[2]{0:T(128)S(1)} %get-tuple-element.9), channel_id=1, replica_groups=mesh['row'=16,'col'=32] {'row','col'}, use_global_device_ids=true, to_apply=%region_5.6 | all-reduce | flops 2 | bytes 16 | tf_op jit(solution)/shard_map/psum | solution.py:108
  252.7 2.6 collective-permute-start.9
  255.3 3.6 collective-permute-start.8
  259.7 1.3 collective-permute-start.10
  261.0 4.0 collective-permute-start.11
  265.0 1.7 collective-permute-done.11
  266.9 101.7 %psum.45 = f32[2]{0:T(128)S(1)} all-reduce(f32[2]{0:T(128)S(1)} %get-tuple-element.7), channel_id=1, replica_groups=mesh['row'=16,'col'=32] {'row','col'}, use_global_device_ids=true, to_apply=%region_7.8 | all-reduce | flops 2 | bytes 16 | tf_op jit(solution)/shard_map/psum | solution.py:140
  368.8 95.3 %psum.46 = f32[2]{0:T(128)S(1)} all-reduce(f32[2]{0:T(128)S(1)} %multiply_reduce_fusion), channel_id=1, replica_groups=mesh['row'=16,'col'=32] {'row','col'}, use_global_device_ids=true, to_apply=%region_9.10 | all-reduce | flops 2 | bytes 16 | tf_op jit(solution)/shard_map/psum | solution.py:108
  464.2 2.6 collective-permute-start.13
  466.8 3.3 collective-permute-start.12
  470.9 1.3 collective-permute-start.14
  472.2 4.0 collective-permute-start.15
  476.5 1.8 collective-permute-done.15
  478.5 101.2 %psum.47 = f32[2]{0:T(128)S(1)} all-reduce(f32[2]{0:T(128)S(1)} %fusion.28), channel_id=1, replica_groups=mesh['row'=16,'col'=32] {'row','col'}, use_global_device_ids=true, to_apply=%region_11.12 | all-reduce | flops 2 | bytes 16 | tf_op jit(solution)/shard_map/psum | solution.py:140
  579.9 2.6 collective-permute-start.17
  582.5 1.3 collective-permute-start.16
  583.8 4.2 collective-permute-done.16
  (63 shorter events, 10.0 us)
Async XLA Ops:
  0.6 0.9 copy-start.3
  1.5 0.8 copy-start.4
  2.4 0.8 copy-start.6
  3.1 0.8 copy-start.5
  4.0 10.1 %collective-permute-start = (f32[5,2,2,128]{3,2,1,0:T(2,128)S(1)}, f32[5,2,2,128]{3,2,1,0:T(2,128)S(1)}, u32[]{:S(2)}, u32[]{:S(2)}) collective-permute-start(f32[5,2,2,128]{3,2,1,0:T(2,128)S(1)} %get-tuple-element.32), channel_id=1, source_target_pairs={{0,32},{32,64},{64,96},{96,128},{128,160},{160,192},{192,224},{224... | collective-permute-start | bytes 30728 | tf_op jit(solution)/shard_map/ppermute | solution.py:23
  8.6 6.3 %collective-permute-start.1 = (f32[5,2,2,128]{3,2,1,0:T(2,128)S(1)}, f32[5,2,2,128]{3,2,1,0:T(2,128)S(1)}, u32[]{:S(2)}, u32[]{:S(2)}) collective-permute-start(f32[5,2,2,128]{3,2,1,0:T(2,128)S(1)} %get-tuple-element.33), channel_id=1, source_target_pairs={{32,0},{64,32},{96,64},{128,96},{160,128},{192,160},{224,192},{256... | collective-permute-start | bytes 30728 | tf_op jit(solution)/shard_map/ppermute | solution.py:25
  15.1 10.2 %collective-permute-start.2 = (f32[5,2,68,2]{3,2,1,0:T(8,128)S(1)}, f32[5,2,68,2]{3,2,1,0:T(8,128)S(1)}, u32[]{:S(2)}, u32[]{:S(2)}) collective-permute-start(f32[5,2,68,2]{3,2,1,0:T(8,128)S(1)} %get-tuple-element.30), channel_id=1, source_target_pairs={{0,1},{1,2},{2,3},{3,4},{4,5},{5,6},{6,7},{7,8},{8,9},{9,10},{10,1... | collective-permute-start | bytes 16328 | tf_op jit(solution)/shard_map/ppermute | solution.py:23
  16.9 12.2 %collective-permute-start.3 = (f32[5,2,68,2]{3,2,1,0:T(8,128)S(1)}, f32[5,2,68,2]{3,2,1,0:T(8,128)S(1)}, u32[]{:S(2)}, u32[]{:S(2)}) collective-permute-start(f32[5,2,68,2]{3,2,1,0:T(8,128)S(1)} %get-tuple-element.31), channel_id=1, source_target_pairs={{1,0},{2,1},{3,2},{4,3},{5,4},{6,5},{7,6},{8,7},{9,8},{10,9},{11,1... | collective-permute-start | bytes 16328 | tf_op jit(solution)/shard_map/ppermute | solution.py:25
  30.4 0.8 copy-start.1
  30.4 0.9 copy-start.2
  31.6 5.6 collective-permute-start.5
  34.2 3.7 collective-permute-start.4
  37.9 6.2 %collective-permute-start.6 = (f32[2,66,1]{2,1,0:T(8,128)S(1)}, f32[2,66,1]{2,1,0:T(8,128)S(1)}, u32[]{:S(2)}, u32[]{:S(2)}) collective-permute-start(f32[2,66,1]{2,1,0:T(8,128)S(1)} %get-tuple-element.38), channel_id=1, source_target_pairs={{1,0},{2,1},{3,2},{4,3},{5,4},{6,5},{7,6},{8,7},{9,8},{10,9},{11,1... | collective-permute-start | bytes 1592 | tf_op jit(solution)/shard_map/ppermute | solution.py:25
  39.2 5.8 collective-permute-start.7
  252.7 6.2 %collective-permute-start.9 = (f32[2,1,128]{2,1,0:T(1,128)S(1)}, f32[2,1,128]{2,1,0:T(1,128)S(1)}, u32[]{:S(2)}, u32[]{:S(2)}) collective-permute-start(f32[2,1,128]{2,1,0:T(1,128)S(1)} %get-tuple-element.44), channel_id=1, source_target_pairs={{32,0},{64,32},{96,64},{128,96},{160,128},{192,160},{224,192},{256... | collective-permute-start | bytes 3080 | tf_op jit(solution)/shard_map/ppermute | solution.py:25
  255.3 4.3 collective-permute-start.8
  259.7 5.3 collective-permute-start.10
  261.0 5.7 collective-permute-start.11
  464.2 5.9 %collective-permute-start.13 = (f32[2,1,128]{2,1,0:T(1,128)S(1)}, f32[2,1,128]{2,1,0:T(1,128)S(1)}, u32[]{:S(2)}, u32[]{:S(2)}) collective-permute-start(f32[2,1,128]{2,1,0:T(1,128)S(1)} %get-tuple-element.42), channel_id=1, source_target_pairs={{32,0},{64,32},{96,64},{128,96},{160,128},{192,160},{224,192},{256... | collective-permute-start | bytes 3080 | tf_op jit(solution)/shard_map/ppermute | solution.py:25
  466.8 4.0 collective-permute-start.12
  470.9 5.6 collective-permute-start.14
  472.2 6.1 %collective-permute-start.15 = (f32[2,66,1]{2,1,0:T(8,128)S(1)}, f32[2,66,1]{2,1,0:T(8,128)S(1)}, u32[]{:S(2)}, u32[]{:S(2)}) collective-permute-start(f32[2,66,1]{2,1,0:T(8,128)S(1)} %get-tuple-element.35), channel_id=1, source_target_pairs={{0,1},{1,2},{2,3},{3,4},{4,5},{5,6},{6,7},{7,8},{8,9},{9,10},{10,1... | collective-permute-start | bytes 1592 | tf_op jit(solution)/shard_map/ppermute | solution.py:23
  579.8 8.2 %copy-start = (f32[2,64,128]{2,1,0:T(8,128)}, f32[2,64,128]{2,1,0:T(8,128)S(1)}, u32[]{:S(2)}) copy-start(f32[2,64,128]{2,1,0:T(8,128)S(1)} %multiply_add_fusion) | copy-start | bytes 196612
  579.9 8.2 %collective-permute-start.17 = (f32[2,1,128]{2,1,0:T(1,128)S(1)}, f32[2,1,128]{2,1,0:T(1,128)S(1)}, u32[]{:S(2)}, u32[]{:S(2)}) collective-permute-start(f32[2,1,128]{2,1,0:T(1,128)S(1)} %slice.398), channel_id=1, source_target_pairs={{32,0},{64,32},{96,64},{128,96},{160,128},{192,160},{224,192},{256... | collective-permute-start | bytes 3080 | tf_op jit(solution)/shard_map/ppermute | solution.py:35
  582.5 5.6 collective-permute-start.16
where the time goes:
time: 591 us; the launch traced here: 589 us
  blocking collectives  505 us (85%)
  starting transfers between devices  50.5 us (9%)
  waiting for transfers between devices  23.6 us (4%)
    psum x3, blocking collectives, squares(): return lax.psum(jnp.sum(residual * residual, axis=(1, 2)), ('row', 'col'))  302 us
    psum x2, blocking collectives, body(): lax.psum(jnp.sum(direction * image, axis=(1, 2)), ('row', 'col'))  203 us
    ppermute x8, starting transfers between devices, extended(): lax.ppermute(tail, axis, [(i, (i + 1) % count) for i in range(ends)])  28.2 us
    ppermute x8, starting transfers between devices, extended(): lax.ppermute(head, axis, [((i + 1) % count, i) for i in range(ends)])  18.4 us
    ppermute x8, waiting for transfers between devices, extended(): lax.ppermute(tail, axis, [(i, (i + 1) % count) for i in range(ends)])  13.6 us
  transfers between devices with their start and end apart: 18, of which 12 were waited for; matrix products, arithmetic and copies ran while one was open for 0% of the time, Pallas kernels for 0%

commit v1 on v0

v1 whole, which is shorter than its diff:
```python
import functools

import jax
import jax.numpy as jnp
from jax import lax
from jax.experimental import pallas as pl
from jax.experimental.pallas import tpu as pltpu
from jax.sharding import PartitionSpec as P

DTDX = 0.5
FRIC = 0.05
G1 = 4.0
CK = DTDX * G1
MESH = pl.DeviceIdType.MESH
F32 = jnp.float32

SURF, UF, VF, RAIN, WET, DEP = range(6)
SHIFT = (0, 8, 16, 48, 56, 64)
PLANES = tuple((f, m) for f in range(6) for m in range(2))
ROWS = 64
TOP = 8
TALL = 80
SIDES = ((1, 0), (-1, 0), (0, 1), (0, -1), (1, 1), (1, -1), (-1, 1), (-1, -1))


def lanes(shape):
    return lax.broadcasted_iota(jnp.int32, shape, len(shape) - 1)


def turn(x, amount):
    return pltpu.roll(x, amount % 128, x.ndim - 1)


def kernel(nrow, ncol, surf_h, u_h, v_h, bed_h, wet_h, rain_h, x_o, nu_o, nv_o,
           field, weti, own_seam, pack_n, pack_s, pack_c, got_n, got_s, got_e, got_w,
           fluxy, kx, ky, wx4, wy4, ub, vb, basis, dxs, dys, out,
           tile1, tile2, tile3, in_sem, out_sem, send_sem, recv_sem, sum_send, sum_recv):
    r0 = lax.axis_index("row")
    c0 = lax.axis_index("col")
    y, core = r0 // 2, r0 % 2
    z, x = c0 // 4, c0 % 4
    q = x * 2 + core

    loads = [
        pltpu.make_async_copy(surf_h, field.at[SURF, 0:2, TOP:TOP + ROWS, :], in_sem.at[0]),
        pltpu.make_async_copy(u_h, field.at[UF, 0:2, TOP:TOP + ROWS, :], in_sem.at[1]),
        pltpu.make_async_copy(v_h, field.at[VF, 0:2, TOP:TOP + ROWS, :], in_sem.at[2]),
        pltpu.make_async_copy(bed_h, field.at[DEP, 0, TOP:TOP + ROWS, :], in_sem.at[3]),
        pltpu.make_async_copy(bed_h, field.at[DEP, 1, TOP:TOP + ROWS, :], in_sem.at[4]),
        pltpu.make_async_copy(wet_h, weti, in_sem.at[5]),
        pltpu.make_async_copy(rain_h, field.at[RAIN, 0:2, TOP:TOP + ROWS, :], in_sem.at[6]),
    ]
    for load in loads:
        load.start()

    def exists(dr, dc):
        ok = None
        for here, step, count in ((r0, dr, nrow), (c0, dc, ncol)):
            if step:
                there = (here + step >= 0) & (here + step < count)
                ok = there if ok is None else ok & there
        return ok

    barrier = pltpu.get_barrier_semaphore()
    groups = [
        [(r0, 4 * ((z + d) % 8) + x) for d in range(1, 8)],
        [(2 * ((y + d) % 8) + core, c0) for d in range(1, 8)],
        [(2 * y + (q + d) % 2, 4 * z + ((q + d) % 8) // 2) for d in range(1, 8)],
    ]
    places = [z, y, q]
    for dr, dc in SIDES:
        @pl.when(exists(dr, dc))
        def _():
            pl.semaphore_signal(barrier, inc=1, device_id=(r0 + dr, c0 + dc), device_id_type=MESH)
    for group in groups:
        for partner in group:
            pl.semaphore_signal(barrier, inc=1, device_id=partner, device_id_type=MESH)

    zero = lambda ref, a, b: ref.__setitem__((slice(a, b), slice(None)), jnp.zeros((b - a, 128), F32))
    for (dr, dc), ref, a, b in (
        ((1, 0), got_n, 0, 48), ((-1, 0), got_s, 0, 48),
        ((0, 1), got_e, 8, 72), ((0, -1), got_w, 8, 72),
        ((1, 1), got_e, 72, 80), ((-1, 1), got_e, 0, 8),
        ((1, -1), got_w, 72, 80), ((-1, -1), got_w, 0, 8),
    ):
        @pl.when(jnp.logical_not(exists(dr, dc)))
        def _():
            zero(ref, a, b)

    for load in loads:
        load.wait()
    for m in range(2):
        field[WET, m, TOP:TOP + ROWS, :] = weti[m].astype(F32)

    for p, (f, m) in enumerate(PLANES):
        pack_n[4 * p:4 * p + 4, :] = field[f, m, TOP + ROWS - 4:TOP + ROWS, :]
        pack_s[4 * p:4 * p + 4, :] = field[f, m, TOP:TOP + 4, :]

    def pack_columns(c, carry):
        row = pl.multiple_of(c * 8, 8)
        lane = lanes((8, 128))
        acc = jnp.zeros((8, 128), F32)
        for f, m in PLANES:
            base = SHIFT[f] + 8 + 24 * m
            rolled = turn(field[f, m, pl.ds(TOP + row, 8), :], base + 4)
            acc = jnp.where((lane >= base) & (lane < base + 8), rolled, acc)
        pack_c[pl.ds(row, 8), :] = acc
        return carry

    lax.fori_loop(0, 8, pack_columns, 0)

    north, south = (r0 + 1 < nrow).astype(jnp.int32), (r0 > 0).astype(jnp.int32)
    east, west = (c0 + 1 < ncol).astype(jnp.int32), (c0 > 0).astype(jnp.int32)
    peers = 21 + (1 + north + south) * (1 + east + west) - 1
    pl.semaphore_wait(barrier, peers)

    def halo(k):
        dr, dc = SIDES[k]
        if dc == 0:
            src, dst = (pack_n, got_s) if dr == 1 else (pack_s, got_n)
        else:
            lands = got_w if dc == 1 else got_e
            if dr == 0:
                src, dst = pack_c, lands.at[8:72, :]
            elif dr == 1:
                src, dst = pack_c.at[56:64, :], lands.at[0:8, :]
            else:
                src, dst = pack_c.at[0:8, :], lands.at[72:80, :]
        return pltpu.make_async_remote_copy(
            src_ref=src, dst_ref=dst, send_sem=send_sem.at[k], recv_sem=recv_sem.at[k],
            device_id=(r0 + dr, c0 + dc), device_id_type=MESH)

    for k, (dr, dc) in enumerate(SIDES):
        @pl.when(exists(dr, dc))
        def _():
            halo(k).start()

    def seam_own(row):
        lane = lanes((8, 128))
        for f in range(6):
            a = field[f, 0, pl.ds(row, 8), :]
            b = field[f, 1, pl.ds(row, 8), :]
            m0 = jnp.where(lane < 12, turn(a, 8), turn(a, 16))
            m1 = jnp.where(lane < 36, turn(b, 32), turn(b, 40))
            own_seam[f, pl.ds(row, 8), :] = jnp.where(lane < 24, m0, m1)

    def seam_body(c, carry):
        seam_own(pl.multiple_of(c * 8 + 8, 8))
        return carry

    lax.fori_loop(0, 8, seam_body, 0)

    for k, (dr, dc) in enumerate(SIDES):
        @pl.when(exists(-dr, -dc))
        def _():
            halo(k).wait_recv()

    for p, (f, m) in enumerate(PLANES):
        field[f, m, 72:76, :] = got_n[4 * p:4 * p + 4, :]
        field[f, m, 4:8, :] = got_s[4 * p:4 * p + 4, :]
    seam_own(0)
    seam_own(72)

    def seam_halo(c, carry):
        row = pl.multiple_of(c * 8, 8)
        lane = lanes((8, 128))
        both = jnp.where((lane & 4) == 0, turn(got_e[pl.ds(row, 8), :], -4), turn(got_w[pl.ds(row, 8), :], 4))
        ghost = ((lane >= 8) & (lane < 16)) | ((lane >= 32) & (lane < 40))
        for f in range(6):
            field[f, 2, pl.ds(row, 8), :] = jnp.where(ghost, turn(both, -SHIFT[f]), own_seam[f, pl.ds(row, 8), :])
        return carry

    lax.fori_loop(0, 10, seam_halo, 0)

    def first(c, carry):
        row = 5 + c * 8

        def at(f, d):
            return field[f, :, pl.ds(row + d, 8), :]

        eta = at(SURF, 0)
        eta_n = at(SURF, 1)
        h = eta + at(DEP, 0)
        h_n = eta_n + at(DEP, 1)
        wet = at(WET, 0)
        u, u_n, u_s = at(UF, 0), at(UF, 1), at(UF, -1)
        v, v_n, v_s = at(VF, 0), at(VF, 1), at(VF, -1)
        wet_x = wet * turn(wet, -1)
        wet_y = wet * at(WET, 1)
        hx = 0.5 * (h + turn(h, -1))
        hy = 0.5 * (h + h_n)
        vs = v + v_s
        vbar = 0.25 * (vs + turn(vs, -1))
        us = u + u_n
        ubar = 0.25 * (us + turn(us, 1))
        adv_u = u * jnp.where(u > 0, u - turn(u, 1), turn(u, -1) - u)
        adv_u = adv_u + vbar * jnp.where(vbar > 0, u - u_s, u_n - u)
        adv_v = v * jnp.where(v > 0, v - v_s, v_n - v)
        adv_v = adv_v + ubar * jnp.where(ubar > 0, v - turn(v, 1), turn(v, -1) - v)
        u_star = wet_x * (u - DTDX * adv_u) / (1.0 + FRIC * jnp.abs(u))
        v_star = wet_y * (v - DTDX * adv_v) / (1.0 + FRIC * jnp.abs(v))
        kx_c = CK * hx * wet_x
        ky_c = CK * hy * wet_y
        drop_x = eta - turn(eta, -1)
        drop_y = eta - eta_n
        fx = DTDX * (hx * u_star) + kx_c * drop_x
        fy = DTDX * (hy * v_star) + ky_c * drop_y
        fluxy[:, pl.ds(row, 8), :] = fy
        kx[:, pl.ds(row, 8), :] = kx_c
        ky[:, pl.ds(row, 8), :] = ky_c
        wx4[:, pl.ds(row, 8), :] = G1 * wet_x
        wy4[:, pl.ds(row, 8), :] = G1 * wet_y
        ub[:, pl.ds(row, 8), :] = u_star + G1 * wet_x * drop_x
        vb[:, pl.ds(row, 8), :] = v_star + G1 * wet_y * drop_y
        basis[0, :, pl.ds(row, 8), :] = (
            at(RAIN, 0) - (fx - turn(fx, 1)) - (fy - fluxy[:, pl.ds(row - 1, 8), :]))
        return carry

    lax.fori_loop(0, 9, first, 0)

    def apply(k, start):
        def body(c, carry):
            row = start + c * 8
            here = pl.ds(row, 8)
            below = pl.ds(row - 1, 8)
            e = basis[k, :, here, :]
            gx = kx[:, here, :] * (e - turn(e, -1))
            gy = ky[:, here, :] * (e - basis[k, :, pl.ds(row + 1, 8), :])
            gs = ky[:, below, :] * (basis[k, :, below, :] - e)
            basis[k + 1, :, here, :] = gx - turn(gx, 1) + (gy - gs)
            return carry

        lax.fori_loop(0, 9, body, 0)

    apply(0, 7)
    apply(1, 8)

    def sums(c, acc):
        row = pl.multiple_of(8 + c * 8, 8)
        here = pl.ds(row, 8)
        v0 = basis[0, :, here, :]
        v1 = basis[1, :, here, :]
        v2 = basis[2, :, here, :]
        dx = turn(v2, -1) - v2
        dy = basis[2, :, pl.ds(row + 1, 8), :] - v2
        terms = (v0 * v0, v0 * v1, v1 * v1, v1 * v2, v2 * v2,
                 kx[:, here, :] * (dx * dx) + ky[:, here, :] * (dy * dy))
        return tuple(a + t for a, t in zip(acc, terms))

    acc = lax.fori_loop(0, 8, sums, tuple(jnp.zeros((3, 8, 128), F32) for _ in range(6)))
    lane = lanes((8, 128))
    sub = lax.broadcasted_iota(jnp.int32, (8, 128), 0)
    own_ok = (lane >= 4) & (lane < 124)
    seam_ok = [((lane >= 4 + 24 * m) & (lane < 8 + 24 * m)) | ((lane >= 16 + 24 * m) & (lane < 20 + 24 * m))
               for m in range(2)]
    rows = []
    for m in range(2):
        table = jnp.zeros((8, 128), F32)
        for k in range(6):
            part = jnp.where(own_ok, acc[k][m], 0.0) + jnp.where(seam_ok[m], acc[k][2], 0.0)
            total = jnp.sum(part, axis=0, keepdims=True)
            table = jnp.where(sub == k, total, table)
        rows.append(table)
    even = (lane & 1) == 0
    tile = jnp.where(even, rows[0] + turn(rows[0], -1), rows[1] + turn(rows[1], 1))
    for amount in (2, 4, 8, 16, 32, 64):
        tile = tile + turn(tile, amount)

    def send_tile(s, slots, value):
        slots[places[s]] = value
        for d in range(7):
            pltpu.make_async_remote_copy(
                src_ref=slots.at[places[s]], dst_ref=slots.at[places[s]],
                send_sem=sum_send.at[s, d], recv_sem=sum_recv.at[s],
                device_id=groups[s][d], device_id_type=MESH).start()

    def take_tiles(s, slots):
        pltpu.make_async_copy(slots.at[0:7], slots.at[0:7], sum_recv.at[s]).wait()
        total = slots[0]
        for k in range(1, 8):
            total = total + slots[k]
        return total

    send_tile(0, tile1, tile)

    def join(c, carry):
        row = pl.multiple_of(8 + c * 8, 8)
        here = pl.ds(row, 8)
        lane = lanes((8, 128))

        def merged(block):
            full = []
            for m in range(2):
                west = turn(block[2], -16 - 24 * m)
                east = turn(block[2], 120 - 24 * m)
                full.append(jnp.where(lane < 4, west, jnp.where(lane >= 124, east, block[m])))
            return full

        wx_c = wx4[:, here, :]
        wy_c = wy4[:, here, :]
        for k in range(3):
            e = basis[k, :, here, :]
            e_n = basis[k, :, pl.ds(row + 1, 8), :]
            for m, value in enumerate(merged(wx_c * (turn(e, -1) - e))):
                dxs[k, m, pl.ds(row - 8, 8), :] = value
            for m, value in enumerate(merged(wy_c * (e_n - e))):
                dys[k, m, pl.ds(row - 8, 8), :] = value
            west_east = merged(e)
            for m in range(2):
                basis[k, m, here, :] = west_east[m]
        for ref, slot in ((ub, 1), (vb, 2)):
            for m, value in enumerate(merged(ref[:, here, :])):
                out[slot, m, pl.ds(row - 8, 8), :] = value
        return carry

    lax.fori_loop(0, 8, join, 0)

    send_tile(1, tile2, take_tiles(0, tile1))
    send_tile(2, tile3, take_tiles(1, tile2))
    total = take_tiles(2, tile3)

    m_ = [total[k:k + 1, :] for k in range(6)]
    s_ = [m_[k] + m_[k + 1] for k in range(5)]
    safe = lambda n, d, ok: jnp.where(ok, n / jnp.where(ok, d, 1.0), 0.0)
    ok0 = s_[0] > 0.0
    l10 = safe(s_[1], s_[0], ok0)
    l20 = safe(s_[2], s_[0], ok0)
    d1 = s_[2] - l10 * s_[1]
    e1 = s_[3] - l10 * s_[2]
    ok1 = d1 > 1e-6 * s_[2]
    l21 = safe(e1, d1, ok1)
    d2 = s_[4] - l20 * s_[2] - l21 * e1
    ok2 = ok1 & (d2 > 1e-6 * s_[4])
    y1 = m_[1] - l10 * m_[0]
    y2 = m_[2] - l20 * m_[0] - l21 * y1
    a2 = safe(y2, d2, ok2)
    a1 = safe(y1, d1, ok1) - l21 * a2
    a0 = safe(m_[0], s_[0], ok0) - l10 * a1 - l20 * a2
    even1 = (lanes((1, 128)) & 1) == 0
    coef = []
    for m in range(2):
        keep = even1 if m == 0 else jnp.logical_not(even1)
        coef.append([jnp.broadcast_to(jnp.where(keep, a, turn(a, 1)), (8, 128)) for a in (a0, a1, a2)])

    def last(c, carry):
        low = pl.multiple_of(c * 8, 8)
        here = pl.ds(low, 8)
        tall = pl.ds(pl.multiple_of(low + 8, 8), 8)
        for m in range(2):
            k0, k1, k2 = coef[m]
            out[0, m, here, :] = (field[SURF, m, tall, :] + k0 * basis[0, m, tall, :]
                                  + k1 * basis[1, m, tall, :] + k2 * basis[2, m, tall, :])
            out[1, m, here, :] = out[1, m, here, :] - (
                k0 * dxs[0, m, here, :] + k1 * dxs[1, m, here, :] + k2 * dxs[2, m, here, :])
            out[2, m, here, :] = out[2, m, here, :] - (
                k0 * dys[0, m, here, :] + k1 * dys[1, m, here, :] + k2 * dys[2, m, here, :])
        return carry

    lax.fori_loop(0, 8, last, 0)
    stores = [pltpu.make_async_copy(out.at[k], ref, out_sem.at[k]) for k, ref in enumerate((x_o, nu_o, nv_o))]
    for store in stores:
        store.start()
    for k, (dr, dc) in enumerate(SIDES):
        @pl.when(exists(dr, dc))
        def _():
            halo(k).wait_send()
    for s, slots in enumerate((tile1, tile2, tile3)):
        for d in range(7):
            pltpu.make_async_remote_copy(
                src_ref=slots.at[places[s]], dst_ref=slots.at[places[s]],
                send_sem=sum_send.at[s, d], recv_sem=sum_recv.at[s],
                device_id=groups[s][d], device_id_type=MESH).wait_send()
    for store in stores:
        store.wait()


def solution(mesh):
    nrow, ncol = mesh.shape["row"], mesh.shape["col"]

    def body(surface, u_face, v_face, bed_depth, wet_mask, rainfall):
        anywhere = pl.BlockSpec(memory_space=pl.ANY)
        vm = lambda *shape: pltpu.VMEM(shape, F32)
        return pl.pallas_call(
            functools.partial(kernel, nrow, ncol),
            out_shape=[jax.ShapeDtypeStruct(surface.shape, F32)] * 3,
            in_specs=[anywhere] * 6,
            out_specs=[anywhere] * 3,
            scratch_shapes=[
                vm(6, 3, TALL, 128),
                pltpu.VMEM((2, ROWS, 128), jnp.int32),
                vm(6, TALL, 128),
                vm(48, 128), vm(48, 128), vm(64, 128),
                vm(48, 128), vm(48, 128), vm(TALL, 128), vm(TALL, 128),
                vm(3, TALL, 128), vm(3, TALL, 128), vm(3, TALL, 128),
                vm(3, TALL, 128), vm(3, TALL, 128), vm(3, TALL, 128), vm(3, TALL, 128),
                vm(3, 3, TALL + 8, 128),
                vm(3, 2, ROWS, 128), vm(3, 2, ROWS, 128), vm(3, 2, ROWS, 128),
                vm(8, 8, 128), vm(8, 8, 128), vm(8, 8, 128),
                pltpu.SemaphoreType.DMA((7,)),
                pltpu.SemaphoreType.DMA((3,)),
                pltpu.SemaphoreType.DMA((8,)),
                pltpu.SemaphoreType.DMA((8,)),
                pltpu.SemaphoreType.DMA((3, 7)),
                pltpu.SemaphoreType.DMA((3,)),
            ],
            compiler_params=pltpu.CompilerParams(collective_id=0, has_side_effects=True),
        )(surface, u_face, v_face, bed_depth, wet_mask, rainfall)

    full = P(None, "row", "col")
    return jax.shard_map(body, mesh=mesh, in_specs=(full, full, full, P("row", "col"), full, full),
                         out_specs=(full, full, full), check_vma=False)
```

time: 591 us -> 44.3 us (0.07)
  blocking collectives: 505 us -> 0 us
  starting transfers between devices: 50.5 us -> 0 us
  Pallas kernels: 0 us -> 40.4 us
  waiting for transfers between devices: 23.6 us -> 0 us
    psum x5 -> x0, blocking collectives: 505 us -> none  [the longest x3 302 us: squares(): return lax.psum(jnp.sum(residual * residual, axis=(1, 2)), ('row', 'col'))]
    ppermute x18 -> x0, starting transfers between devices: 50.5 us -> none  [the longest x8 28.2 us: extended(): lax.ppermute(tail, axis, [(i, (i + 1) % count) for i in range(ends)])]
    pallas_call x0 -> x1, Pallas kernels: none -> 40.4 us  [body(): pl.pallas_call(functools.partial(kernel, nrow, ncol), out_shape=[jax.Shap...]
    ppermute x18 -> x0, waiting for transfers between devices: 23.6 us -> none  [the longest x8 13.6 us: extended(): lax.ppermute(tail, axis, [(i, (i + 1) % count) for i in range(ends)])]
  transfers between devices with their start and end apart: 18 -> 0, of which waited for: 12 -> 0; matrix products, arithmetic and copies ran while one was open for 0% -> 0% of each run, Pallas kernels for 0% -> 0%
where the time goes in v1:
time: 44.3 us; the launch traced here: 44.1 us
  Pallas kernels  40.4 us (91%)
  local copies, waits for them, and re-layouts  3 us (7%)
  between operations  0.65 us (1%)
    pallas_call x1, Pallas kernels, body(): pl.pallas_call(functools.partial(kernel, nrow, ncol), out_shape=[jax.Shap...  40.4 us
    unnamed x7, local copies, waits for them, and re-layouts  3 us

profile of v1, /device:TPU:1, one launch (start us, length us, event | category | flops | bytes accessed | tf_op | source)
XLA Modules:
  0.0 44.1 jit_solution(14977043331562303478)
XLA Ops:
  0.6 40.4 %shard_map.85 = (f32[2,64,128]{2,1,0:T(8,128)}, f32[2,64,128]{2,1,0:T(8,128)}, f32[2,64,128]{2,1,0:T(8,128)}) custom-call(f32[2,64,128]{2,1,0:T(8,128)} %surf_h.1, f32[2,64,128]{2,1,0:T(8,128)} %u_h.1, f32[2,64,128]{2,1,0:T(8,128)} %v_h.1, f32[64,128]{1,0:T(8,128)} %bed_h.1, s32[2,64,128]{2,1,0:T(8,128)} %wet_h.1, f32[2,64,128]{2,1,0:T(8,128)} %rain_h.1), custom_call_target="tpu_custom_call" | custom-call | tf_op jit(solution)/shard_map/pallas_call | solution.py:383
  41.1 0.0 copy-start.1
  41.1 1.5 %copy.12 = f32[2,64,128]{2,1,0:T(8,128)} copy(f32[2,64,128]{2,1,0:T(8,128)} %get-tuple-element.6) | data formatting | bytes 131072
  42.6 0.0 copy-done.1
  42.6 0.0 copy-start
  42.6 0.6 %copy.13 = f32[2,64,128]{2,1,0:T(8,128)} copy(f32[2,64,128]{2,1,0:T(8,128)S(1)} %copy-done.1) | data formatting | bytes 131072
  43.2 0.2 copy-done
  43.5 0.6 %copy.14 = f32[2,64,128]{2,1,0:T(8,128)} copy(f32[2,64,128]{2,1,0:T(8,128)S(1)} %copy-done) | data formatting | bytes 131072
Async XLA Ops:
  41.1 1.5 %copy-start.1 = (f32[2,64,128]{2,1,0:T(8,128)S(1)}, f32[2,64,128]{2,1,0:T(8,128)}, u32[]{:S(2)}) copy-start(f32[2,64,128]{2,1,0:T(8,128)} %get-tuple-element.7) | copy-start | bytes 196612
  42.6 0.9 %copy-start = (f32[2,64,128]{2,1,0:T(8,128)S(1)}, f32[2,64,128]{2,1,0:T(8,128)}, u32[]{:S(2)}) copy-start(f32[2,64,128]{2,1,0:T(8,128)} %get-tuple-element.8) | copy-start | bytes 196612

commit v2 on v1

--- a/solution.py
+++ b/solution.py
@@ -31,10 +31,10 @@
     return pltpu.roll(x, amount % 128, x.ndim - 1)
 
 
-def kernel(nrow, ncol, surf_h, u_h, v_h, bed_h, wet_h, rain_h, x_o, nu_o, nv_o,
+def kernel(nrow, ncol, surf_h, u_h, v_h, bed_h, wet_h, rain_h, out,
            field, weti, own_seam, pack_n, pack_s, pack_c, got_n, got_s, got_e, got_w,
-           fluxy, kx, ky, wx4, wy4, ub, vb, basis, dxs, dys, out,
-           tile1, tile2, tile3, in_sem, out_sem, send_sem, recv_sem, sum_send, sum_recv):
+           fluxy, kx, ky, wx4, wy4, ub, vb, basis, dxs, dys,
+           tile1, tile2, tile3, in_sem, send_sem, recv_sem, sum_send, sum_recv):
     r0 = lax.axis_index("row")
     c0 = lax.axis_index("col")
     y, core = r0 // 2, r0 % 2
@@ -107,7 +107,7 @@
         pack_c[pl.ds(row, 8), :] = acc
         return carry
 
-    lax.fori_loop(0, 8, pack_columns, 0)
+    lax.fori_loop(0, 8, pack_columns, 0, unroll=True)
 
     north, south = (r0 + 1 < nrow).astype(jnp.int32), (r0 > 0).astype(jnp.int32)
     east, west = (c0 + 1 < ncol).astype(jnp.int32), (c0 > 0).astype(jnp.int32)
@@ -148,35 +148,14 @@
         seam_own(pl.multiple_of(c * 8 + 8, 8))
         return carry
 
-    lax.fori_loop(0, 8, seam_body, 0)
-
-    for k, (dr, dc) in enumerate(SIDES):
-        @pl.when(exists(-dr, -dc))
-        def _():
-            halo(k).wait_recv()
-
-    for p, (f, m) in enumerate(PLANES):
-        field[f, m, 72:76, :] = got_n[4 * p:4 * p + 4, :]
-        field[f, m, 4:8, :] = got_s[4 * p:4 * p + 4, :]
-    seam_own(0)
-    seam_own(72)
-
-    def seam_halo(c, carry):
-        row = pl.multiple_of(c * 8, 8)
-        lane = lanes((8, 128))
-        both = jnp.where((lane & 4) == 0, turn(got_e[pl.ds(row, 8), :], -4), turn(got_w[pl.ds(row, 8), :], 4))
-        ghost = ((lane >= 8) & (lane < 16)) | ((lane >= 32) & (lane < 40))
-        for f in range(6):
-            field[f, 2, pl.ds(row, 8), :] = jnp.where(ghost, turn(both, -SHIFT[f]), own_seam[f, pl.ds(row, 8), :])
-        return carry
-
-    lax.fori_loop(0, 10, seam_halo, 0)
-
-    def first(c, carry):
+    lax.fori_loop(0, 8, seam_body, 0, unroll=True)
+
+    def first(blocks, c, open_row=False):
         row = 5 + c * 8
+        here = pl.ds(row, 8)
 
         def at(f, d):
-            return field[f, :, pl.ds(row + d, 8), :]
+            return field[f, blocks, pl.ds(row + d, 8), :]
 
         eta = at(SURF, 0)
         eta_n = at(SURF, 1)
@@ -205,49 +184,95 @@
         drop_y = eta - eta_n
         fx = DTDX * (hx * u_star) + kx_c * drop_x
         fy = DTDX * (hy * v_star) + ky_c * drop_y
-        fluxy[:, pl.ds(row, 8), :] = fy
-        kx[:, pl.ds(row, 8), :] = kx_c
-        ky[:, pl.ds(row, 8), :] = ky_c
-        wx4[:, pl.ds(row, 8), :] = G1 * wet_x
-        wy4[:, pl.ds(row, 8), :] = G1 * wet_y
-        ub[:, pl.ds(row, 8), :] = u_star + G1 * wet_x * drop_x
-        vb[:, pl.ds(row, 8), :] = v_star + G1 * wet_y * drop_y
-        basis[0, :, pl.ds(row, 8), :] = (
-            at(RAIN, 0) - (fx - turn(fx, 1)) - (fy - fluxy[:, pl.ds(row - 1, 8), :]))
+        fluxy[blocks, here, :] = fy
+        kx[blocks, here, :] = kx_c
+        ky[blocks, here, :] = ky_c
+        wx4[blocks, here, :] = G1 * wet_x
+        wy4[blocks, here, :] = G1 * wet_y
+        ub[blocks, here, :] = u_star + G1 * wet_x * drop_x
+        vb[blocks, here, :] = v_star + G1 * wet_y * drop_y
+        rest = at(RAIN, 0) - (fx - turn(fx, 1))
+        basis[0, blocks, here, :] = rest if open_row else rest - (fy - fluxy[blocks, pl.ds(row - 1, 8), :])
+
+    def close_row(blocks, c):
+        row = 5 + c * 8
+        here = pl.ds(row, 8)
+        basis[0, blocks, here, :] = basis[0, blocks, here, :] - (
+            fluxy[blocks, here, :] - fluxy[blocks, pl.ds(row - 1, 8), :])
+
+    def apply(k, blocks, c):
+        row = 7 + k + c * 8
+        here = pl.ds(row, 8)
+        below = pl.ds(row - 1, 8)
+        e = basis[k, blocks, here, :]
+        gx = kx[blocks, here, :] * (e - turn(e, -1))
+        gy = ky[blocks, here, :] * (e - basis[k, blocks, pl.ds(row + 1, 8), :])
+        gs = ky[blocks, below, :] * (basis[k, blocks, below, :] - e)
+        basis[k + 1, blocks, here, :] = gx - turn(gx, 1) + (gy - gs)
+
+    def sums(acc, blocks, c):
+        row = 8 + c * 8
+        here = pl.ds(row, 8)
+        v0 = basis[0, blocks, here, :]
+        v1 = basis[1, blocks, here, :]
+        v2 = basis[2, blocks, here, :]
+        dx = turn(v2, -1) - v2
+        dy = basis[2, blocks, pl.ds(row + 1, 8), :] - v2
+        terms = (v0 * v0, v0 * v1, v1 * v1, v1 * v2, v2 * v2,
+                 kx[blocks, here, :] * (dx * dx) + ky[blocks, here, :] * (dy * dy))
+        return terms if acc is None else tuple(a + t for a, t in zip(acc, terms))
+
+    own, seam = slice(0, 2), slice(2, 3)
+    for c in range(1, 8):
+        first(own, c, open_row=c == 1)
+    for c in range(2, 7):
+        apply(0, own, c)
+    for c in range(2, 6):
+        apply(1, own, c)
+    acc_own = None
+    for c in range(2, 5):
+        acc_own = sums(acc_own, own, c)
+
+    for k, (dr, dc) in enumerate(SIDES):
+        @pl.when(exists(-dr, -dc))
+        def _():
+            halo(k).wait_recv()
+
+    for p, (f, m) in enumerate(PLANES):
+        field[f, m, 72:76, :] = got_n[4 * p:4 * p + 4, :]
+        field[f, m, 4:8, :] = got_s[4 * p:4 * p + 4, :]
+    seam_own(0)
+    seam_own(72)
+
+    def seam_halo(c, carry):
+        row = pl.multiple_of(c * 8, 8)
+        lane = lanes((8, 128))
+        both = jnp.where((lane & 4) == 0, turn(got_e[pl.ds(row, 8), :], -4), turn(got_w[pl.ds(row, 8), :], 4))
+        ghost = ((lane >= 8) & (lane < 16)) | ((lane >= 32) & (lane < 40))
+        for f in range(6):
+            field[f, 2, pl.ds(row, 8), :] = jnp.where(ghost, turn(both, -SHIFT[f]), own_seam[f, pl.ds(row, 8), :])
         return carry
 
-    lax.fori_loop(0, 9, first, 0)
-
-    def apply(k, start):
-        def body(c, carry):
-            row = start + c * 8
-            here = pl.ds(row, 8)
-            below = pl.ds(row - 1, 8)
-            e = basis[k, :, here, :]
-            gx = kx[:, here, :] * (e - turn(e, -1))
-            gy = ky[:, here, :] * (e - basis[k, :, pl.ds(row + 1, 8), :])
-            gs = ky[:, below, :] * (basis[k, :, below, :] - e)
-            basis[k + 1, :, here, :] = gx - turn(gx, 1) + (gy - gs)
-            return carry
-
-        lax.fori_loop(0, 9, body, 0)
-
-    apply(0, 7)
-    apply(1, 8)
-
-    def sums(c, acc):
-        row = pl.multiple_of(8 + c * 8, 8)
-        here = pl.ds(row, 8)
-        v0 = basis[0, :, here, :]
-        v1 = basis[1, :, here, :]
-        v2 = basis[2, :, here, :]
-        dx = turn(v2, -1) - v2
-        dy = basis[2, :, pl.ds(row + 1, 8), :] - v2
-        terms = (v0 * v0, v0 * v1, v1 * v1, v1 * v2, v2 * v2,
-                 kx[:, here, :] * (dx * dx) + ky[:, here, :] * (dy * dy))
-        return tuple(a + t for a, t in zip(acc, terms))
-
-    acc = lax.fori_loop(0, 8, sums, tuple(jnp.zeros((3, 8, 128), F32) for _ in range(6)))
+    lax.fori_loop(0, 10, seam_halo, 0, unroll=True)
+
+    first(own, 0)
+    close_row(own, 1)
+    first(own, 8)
+    for c in range(9):
+        first(seam, c)
+    for c in range(9):
+        apply(0, seam, c)
+    for c in (0, 1, 7, 8):
+        apply(0, own, c)
+    for c in range(9):
+        apply(1, seam, c)
+    for c in (0, 1, 6, 7, 8):
+        apply(1, own, c)
+    acc_seam = None
+    for c in range(8):
+        acc_seam = sums(acc_seam, seam, c)
+    for c in (0, 1, 5, 6, 7):
+        acc_own = sums(acc_own, own, c)
     lane = lanes((8, 128))
     sub = lax.broadcasted_iota(jnp.int32, (8, 128), 0)
     own_ok = (lane >= 4) & (lane < 124)
@@ -257,7 +282,7 @@
     for m in range(2):
         table = jnp.zeros((8, 128), F32)
         for k in range(6):
-            part = jnp.where(own_ok, acc[k][m], 0.0) + jnp.where(seam_ok[m], acc[k][2], 0.0)
+            part = jnp.where(own_ok, acc_own[k][m], 0.0) + jnp.where(seam_ok[m], acc_seam[k][0], 0.0)
             total = jnp.sum(part, axis=0, keepdims=True)
             table = jnp.where(sub == k, total, table)
         rows.append(table)
@@ -313,7 +338,7 @@
                 out[slot, m, pl.ds(row - 8, 8), :] = value
         return carry
 
-    lax.fori_loop(0, 8, join, 0)
+    lax.fori_loop(0, 8, join, 0, unroll=True)
 
     send_tile(1, tile2, take_tiles(0, tile1))
     send_tile(2, tile3, take_tiles(1, tile2))
@@ -356,10 +381,7 @@
                 k0 * dys[0, m, here, :] + k1 * dys[1, m, here, :] + k2 * dys[2, m, here, :])
         return carry
 
-    lax.fori_loop(0, 8, last, 0)
-    stores = [pltpu.make_async_copy(out.at[k], ref, out_sem.at[k]) for k, ref in enumerate((x_o, nu_o, nv_o))]
-    for store in stores:
-        store.start()
+    lax.fori_loop(0, 8, last, 0, unroll=True)
     for k, (dr, dc) in enumerate(SIDES):
         @pl.when(exists(dr, dc))
         def _():
@@ -370,8 +392,14 @@
                 src_ref=slots.at[places[s]], dst_ref=slots.at[places[s]],
                 send_sem=sum_send.at[s, d], recv_sem=sum_recv.at[s],
                 device_id=groups[s][d], device_id_type=MESH).wait_send()
-    for store in stores:
-        store.wait()
+
+
+def hand_over(fields, x_o, nu_o, nv_o, sem):
+    copies = [pltpu.make_async_copy(fields.at[k], ref, sem.at[k]) for k, ref in enumerate((x_o, nu_o, nv_o))]
+    for copy in copies:
+        copy.start()
+    for copy in copies:
+        copy.wait()
 
 
 def solution(mesh):
@@ -380,11 +408,11 @@
     def body(surface, u_face, v_face, bed_depth, wet_mask, rainfall):
         anywhere = pl.BlockSpec(memory_space=pl.ANY)
         vm = lambda *shape: pltpu.VMEM(shape, F32)
-        return pl.pallas_call(
+        fields = pl.pallas_call(
             functools.partial(kernel, nrow, ncol),
-            out_shape=[jax.ShapeDtypeStruct(surface.shape, F32)] * 3,
+            out_shape=jax.ShapeDtypeStruct((3,) + surface.shape, F32),
             in_specs=[anywhere] * 6,
-            out_specs=[anywhere] * 3,
+            out_specs=pl.BlockSpec(memory_space=pltpu.VMEM),
             scratch_shapes=[
                 vm(6, 3, TALL, 128),
                 pltpu.VMEM((2, ROWS, 128), jnp.int32),
@@ -394,17 +422,25 @@
                 vm(3, TALL, 128), vm(3, TALL, 128), vm(3, TALL, 128),
                 vm(3, TALL, 128), vm(3, TALL, 128), vm(3, TALL, 128), vm(3, TALL, 128),
                 vm(3, 3, TALL + 8, 128),
-                vm(3, 2, ROWS, 128), vm(3, 2, ROWS, 128), vm(3, 2, ROWS, 128),
+                vm(3, 2, ROWS, 128), vm(3, 2, ROWS, 128),
                 vm(8, 8, 128), vm(8, 8, 128), vm(8, 8, 128),
                 pltpu.SemaphoreType.DMA((7,)),
-                pltpu.SemaphoreType.DMA((3,)),
                 pltpu.SemaphoreType.DMA((8,)),
                 pltpu.SemaphoreType.DMA((8,)),
                 pltpu.SemaphoreType.DMA((3, 7)),
                 pltpu.SemaphoreType.DMA((3,)),
             ],
-            compiler_params=pltpu.CompilerParams(collective_id=0, has_side_effects=True),
-        )(surface, u_face, v_face, bed_depth, wet_mask, rainfall)
+            compiler_params=pltpu.CompilerParams(collective_id=0, has_side_effects=True,
+                                                 vmem_limit_bytes=8 << 20),
+        )(*(pltpu.with_memory_space_constraint(a, pltpu.HBM) for a in (surface, u_face, v_face, bed_depth, wet_mask, rainfall)))
+        return pl.pallas_call(
+            hand_over,
+            out_shape=[jax.ShapeDtypeStruct(surface.shape, F32)] * 3,
+            in_specs=[anywhere],
+            out_specs=[anywhere] * 3,
+            scratch_shapes=[pltpu.SemaphoreType.DMA((3,))],
+            compiler_params=pltpu.CompilerParams(vmem_limit_bytes=1 << 20),
+        )(fields)
 
     full = P(None, "row", "col")
     return jax.shard_map(body, mesh=mesh, in_specs=(full, full, full, P("row", "col"), full, full),

time: 44.3 us -> 36.1 us (0.81)
  Pallas kernels: 40.4 us -> 35.3 us
  local copies, waits for them, and re-layouts: 3 us -> 0 us
    pallas_call x1 -> x2, Pallas kernels: 40.4 us -> 35.3 us  [the longest x1 34.6 us: body(): pl.pallas_call(functools.partial(kernel, nrow, ncol), out_shape=jax.Shape...]
    unnamed x7 -> x0, local copies, waits for them, and re-layouts: 3 us -> none
where the time goes in v2:
time: 36.1 us; the launch traced here: 35.9 us
  Pallas kernels  35.3 us (98%)
  between operations  0.64 us (2%)
    pallas_call x1, Pallas kernels, body(): pl.pallas_call(functools.partial(kernel, nrow, ncol), out_shape=jax.Shape...  34.6 us

profile of v2, /device:TPU:1, one launch (start us, length us, event | category | flops | bytes accessed | tf_op | source)
XLA Modules:
  0.0 35.9 jit_solution(9711982136041516890)
XLA Ops:
  0.6 34.6 %shard_map.85.fields = f32[3,2,64,128]{3,2,1,0:T(8,128)S(1)} custom-call(f32[2,64,128]{2,1,0:T(8,128)} %surf_h.1, f32[2,64,128]{2,1,0:T(8,128)} %u_h.1, f32[2,64,128]{2,1,0:T(8,128)} %v_h.1, f32[64,128]{1,0:T(8,128)} %bed_h.1, s32[2,64,128]{2,1,0:T(8,128)} %wet_h.1, f32[2,64,128]{2,1,0:T(8,128)} %rain_h.1), custom_call_target="tpu_custom_call" | custom-call | tf_op jit(solution)/shard_map/pallas_call | solution.py:411
  35.2 0.7 %shard_map.86 = (f32[2,64,128]{2,1,0:T(8,128)}, f32[2,64,128]{2,1,0:T(8,128)}, f32[2,64,128]{2,1,0:T(8,128)}) custom-call(f32[3,2,64,128]{3,2,1,0:T(8,128)S(1)} %shard_map.85.fields), custom_call_target="tpu_custom_call" | custom-call | tf_op jit(solution)/shard_map/pallas_call | solution.py:436

commit v3 on v2

--- a/solution.py
+++ b/solution.py
@@ -62,12 +62,13 @@
         return ok
 
     barrier = pltpu.get_barrier_semaphore()
+    places = [q, z, y]
+    others = [[d + (d >= place).astype(jnp.int32) for d in range(7)] for place in places]
     groups = [
-        [(r0, 4 * ((z + d) % 8) + x) for d in range(1, 8)],
-        [(2 * ((y + d) % 8) + core, c0) for d in range(1, 8)],
-        [(2 * y + (q + d) % 2, 4 * z + ((q + d) % 8) // 2) for d in range(1, 8)],
+        [(2 * y + t % 2, 4 * z + t // 2) for t in others[0]],
+        [(r0, 4 * t + x) for t in others[1]],
+        [(2 * t + core, c0) for t in others[2]],
     ]
-    places = [z, y, q]
     for dr, dc in SIDES:
         @pl.when(exists(dr, dc))
         def _():
@@ -274,22 +275,15 @@
     for c in (0, 1, 5, 6, 7):
         acc_own = sums(acc_own, own, c)
     lane = lanes((8, 128))
-    sub = lax.broadcasted_iota(jnp.int32, (8, 128), 0)
     own_ok = (lane >= 4) & (lane < 124)
     seam_ok = [((lane >= 4 + 24 * m) & (lane < 8 + 24 * m)) | ((lane >= 16 + 24 * m) & (lane < 20 + 24 * m))
                for m in range(2)]
-    rows = []
+    spread = jnp.zeros((8, 128), F32)
     for m in range(2):
-        table = jnp.zeros((8, 128), F32)
         for k in range(6):
             part = jnp.where(own_ok, acc_own[k][m], 0.0) + jnp.where(seam_ok[m], acc_seam[k][0], 0.0)
-            total = jnp.sum(part, axis=0, keepdims=True)
-            table = jnp.where(sub == k, total, table)
-        rows.append(table)
-    even = (lane & 1) == 0
-    tile = jnp.where(even, rows[0] + turn(rows[0], -1), rows[1] + turn(rows[1], 1))
-    for amount in (2, 4, 8, 16, 32, 64):
-        tile = tile + turn(tile, amount)
+            spread = jnp.where(lane == 2 * k + m, jnp.sum(part, axis=1, keepdims=True), spread)
+    tile = jnp.sum(spread, axis=0, keepdims=True)
 
     def send_tile(s, slots, value):
         slots[places[s]] = value
@@ -344,7 +338,7 @@
     send_tile(2, tile3, take_tiles(1, tile2))
     total = take_tiles(2, tile3)
 
-    m_ = [total[k:k + 1, :] for k in range(6)]
+    m_ = [turn(total, -2 * k) for k in range(6)]
     s_ = [m_[k] + m_[k + 1] for k in range(5)]
     safe = lambda n, d, ok: jnp.where(ok, n / jnp.where(ok, d, 1.0), 0.0)
     ok0 = s_[0] > 0.0
@@ -361,11 +355,7 @@
     a2 = safe(y2, d2, ok2)
     a1 = safe(y1, d1, ok1) - l21 * a2
     a0 = safe(m_[0], s_[0], ok0) - l10 * a1 - l20 * a2
-    even1 = (lanes((1, 128)) & 1) == 0
-    coef = []
-    for m in range(2):
-        keep = even1 if m == 0 else jnp.logical_not(even1)
-        coef.append([jnp.broadcast_to(jnp.where(keep, a, turn(a, 1)), (8, 128)) for a in (a0, a1, a2)])
+    coef = [[jnp.broadcast_to(a[:, m:m + 1], (8, 128)) for a in (a0, a1, a2)] for m in range(2)]
 
     def last(c, carry):
         low = pl.multiple_of(c * 8, 8)
@@ -423,7 +413,7 @@
                 vm(3, TALL, 128), vm(3, TALL, 128), vm(3, TALL, 128), vm(3, TALL, 128),
                 vm(3, 3, TALL + 8, 128),
                 vm(3, 2, ROWS, 128), vm(3, 2, ROWS, 128),
-                vm(8, 8, 128), vm(8, 8, 128), vm(8, 8, 128),
+                vm(8, 1, 128), vm(8, 1, 128), vm(8, 1, 128),
                 pltpu.SemaphoreType.DMA((7,)),
                 pltpu.SemaphoreType.DMA((8,)),
                 pltpu.SemaphoreType.DMA((8,)),

time: 36.1 us -> 35.2 us (0.975)
  the two profiles are of different devices: /device:TPU:1 before, /device:TPU:2 now
where the time goes in v3:
time: 35.2 us; the launch traced here: 35.1 us
  Pallas kernels  34.4 us (98%)
  between operations  0.64 us (2%)
    pallas_call x1, Pallas kernels, body(): pl.pallas_call(functools.partial(kernel, nrow, ncol), out_shape=jax.Shape...  33.7 us

profile of v3, /device:TPU:2, one launch (start us, length us, event | category | flops | bytes accessed | tf_op | source)
XLA Modules:
  0.0 35.1 jit_solution(56615776421978225)
XLA Ops:
  0.6 33.7 %shard_map.85.fields = f32[3,2,64,128]{3,2,1,0:T(8,128)S(1)} custom-call(f32[2,64,128]{2,1,0:T(8,128)} %surf_h.1, f32[2,64,128]{2,1,0:T(8,128)} %u_h.1, f32[2,64,128]{2,1,0:T(8,128)} %v_h.1, f32[64,128]{1,0:T(8,128)} %bed_h.1, s32[2,64,128]{2,1,0:T(8,128)} %wet_h.1, f32[2,64,128]{2,1,0:T(8,128)} %rain_h.1), custom_call_target="tpu_custom_call" | custom-call | tf_op jit(solution)/shard_map/pallas_call | solution.py:401
  34.4 0.7 %shard_map.86 = (f32[2,64,128]{2,1,0:T(8,128)}, f32[2,64,128]{2,1,0:T(8,128)}, f32[2,64,128]{2,1,0:T(8,128)}) custom-call(f32[3,2,64,128]{3,2,1,0:T(8,128)S(1)} %shard_map.85.fields), custom_call_target="tpu_custom_call" | custom-call | tf_op jit(solution)/shard_map/pallas_call | solution.py:426

commit v4 on v3

--- a/solution.py
+++ b/solution.py
@@ -278,12 +278,19 @@
     own_ok = (lane >= 4) & (lane < 124)
     seam_ok = [((lane >= 4 + 24 * m) & (lane < 8 + 24 * m)) | ((lane >= 16 + 24 * m) & (lane < 20 + 24 * m))
                for m in range(2)]
-    spread = jnp.zeros((8, 128), F32)
+    sub = lax.broadcasted_iota(jnp.int32, (8, 128), 0)
+    tables = []
     for m in range(2):
+        table = jnp.zeros((8, 128), F32)
         for k in range(6):
             part = jnp.where(own_ok, acc_own[k][m], 0.0) + jnp.where(seam_ok[m], acc_seam[k][0], 0.0)
-            spread = jnp.where(lane == 2 * k + m, jnp.sum(part, axis=1, keepdims=True), spread)
-    tile = jnp.sum(spread, axis=0, keepdims=True)
+            table = jnp.where(sub == k, jnp.sum(part, axis=0, keepdims=True), table)
+        tables.append(table)
+    even = (lane & 1) == 0
+    both_m = jnp.where(even, tables[0] + turn(tables[0], -1), tables[1] + turn(tables[1], 1))
+    for amount in (2, 4, 8, 16, 32, 64):
+        both_m = both_m + turn(both_m, amount)
+    tile = jnp.sum(jnp.where(lane // 2 == sub, both_m, 0.0), axis=0, keepdims=True)
 
     def send_tile(s, slots, value):
         slots[places[s]] = value
@@ -332,7 +339,7 @@
                 out[slot, m, pl.ds(row - 8, 8), :] = value
         return carry
 
-    lax.fori_loop(0, 8, join, 0, unroll=True)
+    lax.fori_loop(0, 8, join, 0, unroll=2)
 
     send_tile(1, tile2, take_tiles(0, tile1))
     send_tile(2, tile3, take_tiles(1, tile2))

time: 35.2 us -> 34.5 us (0.980)
  Pallas kernels: 34.4 us -> 33.7 us
    pallas_call x1, Pallas kernels: 33.7 us -> 33 us  [body(): pl.pallas_call(functools.partial(kernel, nrow, ncol), out_shape=jax.Shape...]
where the time goes in v4:
time: 34.5 us; the launch traced here: 34.3 us
  Pallas kernels  33.7 us (98%)
  between operations  0.64 us (2%)
    pallas_call x1, Pallas kernels, body(): pl.pallas_call(functools.partial(kernel, nrow, ncol), out_shape=jax.Shape...  33 us
    pallas_call x1, Pallas kernels, body(): pl.pallas_call(hand_over, out_shape=[jax.ShapeDtypeStruct(surface.shape,...  0.7 us

profile of v4, /device:TPU:2, one launch (start us, length us, event | category | flops | bytes accessed | tf_op | source)
XLA Modules:
  0.0 34.3 jit_solution(1335901153439087562)
XLA Ops:
  0.6 33.0 %shard_map.85.fields = f32[3,2,64,128]{3,2,1,0:T(8,128)S(1)} custom-call(f32[2,64,128]{2,1,0:T(8,128)} %surf_h.1, f32[2,64,128]{2,1,0:T(8,128)} %u_h.1, f32[2,64,128]{2,1,0:T(8,128)} %v_h.1, f32[64,128]{1,0:T(8,128)} %bed_h.1, s32[2,64,128]{2,1,0:T(8,128)} %wet_h.1, f32[2,64,128]{2,1,0:T(8,128)} %rain_h.1), custom_call_target="tpu_custom_call" | custom-call | tf_op jit(solution)/shard_map/pallas_call | solution.py:408
  33.6 0.7 %shard_map.86 = (f32[2,64,128]{2,1,0:T(8,128)}, f32[2,64,128]{2,1,0:T(8,128)}, f32[2,64,128]{2,1,0:T(8,128)}) custom-call(f32[3,2,64,128]{3,2,1,0:T(8,128)S(1)} %shard_map.85.fields), custom_call_target="tpu_custom_call" | custom-call | tf_op jit(solution)/shard_map/pallas_call | solution.py:433

commit v5 on v4

--- a/solution.py
+++ b/solution.py
@@ -20,7 +20,7 @@
 ROWS = 64
 TOP = 8
 TALL = 80
-SIDES = ((1, 0), (-1, 0), (0, 1), (0, -1), (1, 1), (1, -1), (-1, 1), (-1, -1))
+SIDES = ((1, 1), (1, -1), (-1, 1), (-1, -1), (0, 1), (0, -1), (1, 0), (-1, 0))
 
 
 def lanes(shape):
@@ -34,7 +34,7 @@
 def kernel(nrow, ncol, surf_h, u_h, v_h, bed_h, wet_h, rain_h, out,
            field, weti, own_seam, pack_n, pack_s, pack_c, got_n, got_s, got_e, got_w,
            fluxy, kx, ky, wx4, wy4, ub, vb, basis, dxs, dys,
-           tile1, tile2, tile3, in_sem, send_sem, recv_sem, sum_send, sum_recv):
+           tile1, tile2, tile3, in_sem, send_sem, recv_sem, sum_send, sum_recv, word):
     r0 = lax.axis_index("row")
     c0 = lax.axis_index("col")
     y, core = r0 // 2, r0 % 2
@@ -50,8 +50,6 @@
         pltpu.make_async_copy(wet_h, weti, in_sem.at[5]),
         pltpu.make_async_copy(rain_h, field.at[RAIN, 0:2, TOP:TOP + ROWS, :], in_sem.at[6]),
     ]
-    for load in loads:
-        load.start()
 
     def exists(dr, dc):
         ok = None
@@ -69,13 +67,18 @@
         [(r0, 4 * t + x) for t in others[1]],
         [(2 * t + core, c0) for t in others[2]],
     ]
+
+    def ring(e):
+        return [place for d in (e, 8 - e) for place in ((2 * ((y + d) % 8) + core, c0), (r0, 4 * ((z + d) % 8) + x))]
+
     for dr, dc in SIDES:
         @pl.when(exists(dr, dc))
         def _():
             pl.semaphore_signal(barrier, inc=1, device_id=(r0 + dr, c0 + dc), device_id_type=MESH)
-    for group in groups:
-        for partner in group:
-            pl.semaphore_signal(barrier, inc=1, device_id=partner, device_id_type=MESH)
+    for partner in groups[0] + ring(1):
+        pl.semaphore_signal(barrier, inc=1, device_id=partner, device_id_type=MESH)
+    for load in loads:
+        load.start()
 
     zero = lambda ref, a, b: ref.__setitem__((slice(a, b), slice(None)), jnp.zeros((b - a, 128), F32))
     for (dr, dc), ref, a, b in (
@@ -93,10 +96,6 @@
     for m in range(2):
         field[WET, m, TOP:TOP + ROWS, :] = weti[m].astype(F32)
 
-    for p, (f, m) in enumerate(PLANES):
-        pack_n[4 * p:4 * p + 4, :] = field[f, m, TOP + ROWS - 4:TOP + ROWS, :]
-        pack_s[4 * p:4 * p + 4, :] = field[f, m, TOP:TOP + 4, :]
-
     def pack_columns(c, carry):
         row = pl.multiple_of(c * 8, 8)
         lane = lanes((8, 128))
@@ -112,7 +111,7 @@
 
     north, south = (r0 + 1 < nrow).astype(jnp.int32), (r0 > 0).astype(jnp.int32)
     east, west = (c0 + 1 < ncol).astype(jnp.int32), (c0 > 0).astype(jnp.int32)
-    peers = 21 + (1 + north + south) * (1 + east + west) - 1
+    peers = 11 + (1 + north + south) * (1 + east + west) - 1
     pl.semaphore_wait(barrier, peers)
 
     def halo(k):
@@ -131,10 +130,19 @@
             src_ref=src, dst_ref=dst, send_sem=send_sem.at[k], recv_sem=recv_sem.at[k],
             device_id=(r0 + dr, c0 + dc), device_id_type=MESH)
 
-    for k, (dr, dc) in enumerate(SIDES):
-        @pl.when(exists(dr, dc))
-        def _():
-            halo(k).start()
+    def send(some):
+        for k in some:
+            @pl.when(exists(*SIDES[k]))
+            def _():
+                halo(k).start()
+
+    send(range(6))
+    for p, (f, m) in enumerate(PLANES):
+        pack_n[4 * p:4 * p + 4, :] = field[f, m, TOP + ROWS - 4:TOP + ROWS, :]
+        pack_s[4 * p:4 * p + 4, :] = field[f, m, TOP:TOP + 4, :]
+    send(range(6, 8))
+    for partner in ring(1):
+        pl.semaphore_signal(word.at[0], inc=1, device_id=partner, device_id_type=MESH)
 
     def seam_own(row):
         lane = lanes((8, 128))
@@ -234,16 +242,35 @@
     for c in range(2, 5):
         acc_own = sums(acc_own, own, c)
 
-    for k, (dr, dc) in enumerate(SIDES):
-        @pl.when(exists(-dr, -dc))
-        def _():
-            halo(k).wait_recv()
-
+    def receive(some):
+        for k in some:
+            dr, dc = SIDES[k]
+
+            @pl.when(exists(-dr, -dc))
+            def _():
+                halo(k).wait_recv()
+
+    pl.semaphore_wait(word.at[0], 4)
+    for partner in ring(2):
+        pl.semaphore_signal(word.at[1], inc=1, device_id=partner, device_id_type=MESH)
+    receive(range(6, 8))
     for p, (f, m) in enumerate(PLANES):
         field[f, m, 72:76, :] = got_n[4 * p:4 * p + 4, :]
         field[f, m, 4:8, :] = got_s[4 * p:4 * p + 4, :]
     seam_own(0)
     seam_own(72)
+
+    first(own, 0)
+    close_row(own, 1)
+    first(own, 8)
+    for c in (0, 1, 7, 8):
+        apply(0, own, c)
+    for c in (0, 1, 6, 7, 8):
+        apply(1, own, c)
+    for c in (0, 1, 5, 6, 7):
+        acc_own = sums(acc_own, own, c)
+
+    receive(range(6))
 
     def seam_halo(c, carry):
         row = pl.multiple_of(c * 8, 8)
@@ -256,24 +283,15 @@
 
     lax.fori_loop(0, 10, seam_halo, 0, unroll=True)
 
-    first(own, 0)
-    close_row(own, 1)
-    first(own, 8)
     for c in range(9):
         first(seam, c)
     for c in range(9):
         apply(0, seam, c)
-    for c in (0, 1, 7, 8):
-        apply(0, own, c)
     for c in range(9):
         apply(1, seam, c)
-    for c in (0, 1, 6, 7, 8):
-        apply(1, own, c)
     acc_seam = None
     for c in range(8):
         acc_seam = sums(acc_seam, seam, c)
-    for c in (0, 1, 5, 6, 7):
-        acc_own = sums(acc_own, own, c)
     lane = lanes((8, 128))
     own_ok = (lane >= 4) & (lane < 124)
     seam_ok = [((lane >= 4 + 24 * m) & (lane < 8 + 24 * m)) | ((lane >= 16 + 24 * m) & (lane < 20 + 24 * m))
@@ -288,8 +306,8 @@
         tables.append(table)
     even = (lane & 1) == 0
     both_m = jnp.where(even, tables[0] + turn(tables[0], -1), tables[1] + turn(tables[1], 1))
-    for amount in (2, 4, 8, 16, 32, 64):
-        both_m = both_m + turn(both_m, amount)
+    for step in (2, 8, 32):
+        both_m = (both_m + turn(both_m, step)) + (turn(both_m, 2 * step) + turn(both_m, 3 * step))
     tile = jnp.sum(jnp.where(lane // 2 == sub, both_m, 0.0), axis=0, keepdims=True)
 
     def send_tile(s, slots, value):
@@ -341,6 +359,7 @@
 
     lax.fori_loop(0, 8, join, 0, unroll=2)
 
+    pl.semaphore_wait(word.at[1], 4)
     send_tile(1, tile2, take_tiles(0, tile1))
     send_tile(2, tile3, take_tiles(1, tile2))
     total = take_tiles(2, tile3)
@@ -426,6 +445,7 @@
                 pltpu.SemaphoreType.DMA((8,)),
                 pltpu.SemaphoreType.DMA((3, 7)),
                 pltpu.SemaphoreType.DMA((3,)),
+                pltpu.SemaphoreType.REGULAR((2,)),
             ],
             compiler_params=pltpu.CompilerParams(collective_id=0, has_side_effects=True,
                                                  vmem_limit_bytes=8 << 20),

time: 34.5 us -> 32.9 us (0.954)
  the two profiles are of different devices: /device:TPU:2 before, /device:TPU:1 now
where the time goes in v5:
time: 32.9 us; the launch traced here: 32.5 us
  Pallas kernels  31.8 us (97%)
  between operations  0.64 us (2%)
    pallas_call x1, Pallas kernels, body(): pl.pallas_call(functools.partial(kernel, nrow, ncol), out_shape=jax.Shape...  31.1 us
    pallas_call x1, Pallas kernels, body(): pl.pallas_call(hand_over, out_shape=[jax.ShapeDtypeStruct(surface.shape,...  0.7 us

profile of v5, /device:TPU:1, one launch (start us, length us, event | category | flops | bytes accessed | tf_op | source)
XLA Modules:
  0.0 32.5 jit_solution(12131137462674857318)
XLA Ops:
  0.6 31.1 %shard_map.85.fields = f32[3,2,64,128]{3,2,1,0:T(8,128)S(1)} custom-call(f32[2,64,128]{2,1,0:T(8,128)} %surf_h.1, f32[2,64,128]{2,1,0:T(8,128)} %u_h.1, f32[2,64,128]{2,1,0:T(8,128)} %v_h.1, f32[64,128]{1,0:T(8,128)} %bed_h.1, s32[2,64,128]{2,1,0:T(8,128)} %wet_h.1, f32[2,64,128]{2,1,0:T(8,128)} %rain_h.1), custom_call_target="tpu_custom_call" | custom-call | tf_op jit(solution)/shard_map/pallas_call | solution.py:427
  31.8 0.7 %shard_map.86 = (f32[2,64,128]{2,1,0:T(8,128)}, f32[2,64,128]{2,1,0:T(8,128)}, f32[2,64,128]{2,1,0:T(8,128)}) custom-call(f32[3,2,64,128]{3,2,1,0:T(8,128)S(1)} %shard_map.85.fields), custom_call_target="tpu_custom_call" | custom-call | tf_op jit(solution)/shard_map/pallas_call | solution.py:453

commit v6 on v5

--- a/solution.py
+++ b/solution.py
@@ -34,7 +34,7 @@
 def kernel(nrow, ncol, surf_h, u_h, v_h, bed_h, wet_h, rain_h, out,
            field, weti, own_seam, pack_n, pack_s, pack_c, got_n, got_s, got_e, got_w,
            fluxy, kx, ky, wx4, wy4, ub, vb, basis, dxs, dys,
-           tile1, tile2, tile3, in_sem, send_sem, recv_sem, sum_send, sum_recv, word):
+           tile1, tile2, in_sem, send_sem, recv_sem, sum_send, sum_recv, word):
     r0 = lax.axis_index("row")
     c0 = lax.axis_index("col")
     y, core = r0 // 2, r0 % 2
@@ -60,13 +60,11 @@
         return ok
 
     barrier = pltpu.get_barrier_semaphore()
-    places = [q, z, y]
-    others = [[d + (d >= place).astype(jnp.int32) for d in range(7)] for place in places]
-    groups = [
-        [(2 * y + t % 2, 4 * z + t // 2) for t in others[0]],
-        [(r0, 4 * t + x) for t in others[1]],
-        [(2 * t + core, c0) for t in others[2]],
-    ]
+    near = [(q + d) % 8 for d in range(1, 8)]
+    near = [(2 * y + t % 2, 4 * z + t // 2) for t in near]
+    places = [r0, c0]
+    others = [[d + (d >= place).astype(jnp.int32) for d in range(n - 1)] for place, n in zip(places, (nrow, ncol))]
+    groups = [[(t, c0) for t in others[0]], [(r0, t) for t in others[1]]]
 
     def ring(e):
         return [place for d in (e, 8 - e) for place in ((2 * ((y + d) % 8) + core, c0), (r0, 4 * ((z + d) % 8) + x))]
@@ -75,7 +73,7 @@
         @pl.when(exists(dr, dc))
         def _():
             pl.semaphore_signal(barrier, inc=1, device_id=(r0 + dr, c0 + dc), device_id_type=MESH)
-    for partner in groups[0] + ring(1):
+    for partner in near + ring(1):
         pl.semaphore_signal(barrier, inc=1, device_id=partner, device_id_type=MESH)
     for load in loads:
         load.start()
@@ -270,6 +268,9 @@
     for c in (0, 1, 5, 6, 7):
         acc_own = sums(acc_own, own, c)
 
+    pl.semaphore_wait(word.at[1], 4)
+    for partner in ring(1):
+        pl.semaphore_signal(word.at[2], inc=1, device_id=partner, device_id_type=MESH)
     receive(range(6))
 
     def seam_halo(c, carry):
@@ -312,19 +313,24 @@
 
     def send_tile(s, slots, value):
         slots[places[s]] = value
-        for d in range(7):
+        for partner in groups[s]:
             pltpu.make_async_remote_copy(
                 src_ref=slots.at[places[s]], dst_ref=slots.at[places[s]],
-                send_sem=sum_send.at[s, d], recv_sem=sum_recv.at[s],
-                device_id=groups[s][d], device_id_type=MESH).start()
+                send_sem=sum_send.at[s], recv_sem=sum_recv.at[s],
+                device_id=partner, device_id_type=MESH).start()
+
+    def wait_all(slots, sem):
+        rest = slots.at[0:slots.shape[0] - 1]
+        pltpu.make_async_copy(rest, rest, sem).wait()
 
     def take_tiles(s, slots):
-        pltpu.make_async_copy(slots.at[0:7], slots.at[0:7], sum_recv.at[s]).wait()
-        total = slots[0]
-        for k in range(1, 8):
-            total = total + slots[k]
-        return total
-
+        wait_all(slots, sum_recv.at[s])
+        terms = [slots[k] for k in range(slots.shape[0])]
+        while len(terms) > 1:
+            terms = [a + b for a, b in zip(terms[::2], terms[1::2])]
+        return terms[0]
+
+    pl.semaphore_wait(word.at[2], 4)
     send_tile(0, tile1, tile)
 
     def join(c, carry):
@@ -359,10 +365,8 @@
 
     lax.fori_loop(0, 8, join, 0, unroll=2)
 
-    pl.semaphore_wait(word.at[1], 4)
     send_tile(1, tile2, take_tiles(0, tile1))
-    send_tile(2, tile3, take_tiles(1, tile2))
-    total = take_tiles(2, tile3)
+    total = take_tiles(1, tile2)
 
     m_ = [turn(total, -2 * k) for k in range(6)]
     s_ = [m_[k] + m_[k + 1] for k in range(5)]
@@ -402,12 +406,8 @@
         @pl.when(exists(dr, dc))
         def _():
             halo(k).wait_send()
-    for s, slots in enumerate((tile1, tile2, tile3)):
-        for d in range(7):
-            pltpu.make_async_remote_copy(
-                src_ref=slots.at[places[s]], dst_ref=slots.at[places[s]],
-                send_sem=sum_send.at[s, d], recv_sem=sum_recv.at[s],
-                device_id=groups[s][d], device_id_type=MESH).wait_send()
+    for s, slots in enumerate((tile1, tile2)):
+        wait_all(slots, sum_send.at[s])
 
 
 def hand_over(fields, x_o, nu_o, nv_o, sem):
@@ -439,13 +439,13 @@
                 vm(3, TALL, 128), vm(3, TALL, 128), vm(3, TALL, 128), vm(3, TALL, 128),
                 vm(3, 3, TALL + 8, 128),
                 vm(3, 2, ROWS, 128), vm(3, 2, ROWS, 128),
-                vm(8, 1, 128), vm(8, 1, 128), vm(8, 1, 128),
+                vm(nrow, 1, 128), vm(ncol, 1, 128),
                 pltpu.SemaphoreType.DMA((7,)),
                 pltpu.SemaphoreType.DMA((8,)),
                 pltpu.SemaphoreType.DMA((8,)),
-                pltpu.SemaphoreType.DMA((3, 7)),
-                pltpu.SemaphoreType.DMA((3,)),
-                pltpu.SemaphoreType.REGULAR((2,)),
+                pltpu.SemaphoreType.DMA((2,)),
+                pltpu.SemaphoreType.DMA((2,)),
+                pltpu.SemaphoreType.REGULAR((3,)),
             ],
             compiler_params=pltpu.CompilerParams(collective_id=0, has_side_effects=True,
                                                  vmem_limit_bytes=8 << 20),

time: 32.9 us -> 31.3 us (0.951)
  Pallas kernels: 31.8 us -> 30.5 us
    pallas_call x1, Pallas kernels: 31.1 us -> 29.8 us  [body(): pl.pallas_call(functools.partial(kernel, nrow, ncol), out_shape=jax.Shape...]
where the time goes in v6:
time: 31.3 us; the launch traced here: 31.1 us
  Pallas kernels  30.5 us (97%)
  between operations  0.64 us (2%)
    pallas_call x1, Pallas kernels, body(): pl.pallas_call(functools.partial(kernel, nrow, ncol), out_shape=jax.Shape...  29.8 us
    pallas_call x1, Pallas kernels, body(): pl.pallas_call(hand_over, out_shape=[jax.ShapeDtypeStruct(surface.shape,...  0.7 us

profile of v6, /device:TPU:1, one launch (start us, length us, event | category | flops | bytes accessed | tf_op | source)
XLA Modules:
  0.0 31.1 jit_solution(13323435365841413005)
XLA Ops:
  0.6 29.8 %shard_map.85.fields = f32[3,2,64,128]{3,2,1,0:T(8,128)S(1)} custom-call(f32[2,64,128]{2,1,0:T(8,128)} %surf_h.1, f32[2,64,128]{2,1,0:T(8,128)} %u_h.1, f32[2,64,128]{2,1,0:T(8,128)} %v_h.1, f32[64,128]{1,0:T(8,128)} %bed_h.1, s32[2,64,128]{2,1,0:T(8,128)} %wet_h.1, f32[2,64,128]{2,1,0:T(8,128)} %rain_h.1), custom_call_target="tpu_custom_call" | custom-call | tf_op jit(solution)/shard_map/pallas_call | solution.py:427
  30.4 0.7 %shard_map.86 = (f32[2,64,128]{2,1,0:T(8,128)}, f32[2,64,128]{2,1,0:T(8,128)}, f32[2,64,128]{2,1,0:T(8,128)}) custom-call(f32[3,2,64,128]{3,2,1,0:T(8,128)S(1)} %shard_map.85.fields), custom_call_target="tpu_custom_call" | custom-call | tf_op jit(solution)/shard_map/pallas_call | solution.py:453

commit v7 on v6

--- a/solution.py
+++ b/solution.py
@@ -73,10 +73,12 @@
         @pl.when(exists(dr, dc))
         def _():
             pl.semaphore_signal(barrier, inc=1, device_id=(r0 + dr, c0 + dc), device_id_type=MESH)
-    for partner in near + ring(1):
+    for partner in ring(1):
         pl.semaphore_signal(barrier, inc=1, device_id=partner, device_id_type=MESH)
     for load in loads:
         load.start()
+    for partner in near:
+        pl.semaphore_signal(barrier, inc=1, device_id=partner, device_id_type=MESH)
 
     zero = lambda ref, a, b: ref.__setitem__((slice(a, b), slice(None)), jnp.zeros((b - a, 128), F32))
     for (dr, dc), ref, a, b in (

time: 31.3 us -> 31.3 us (level)
  no operation moved by 1% of the time
where the time goes in v7:
time: 31.3 us; the launch traced here: 31.1 us
  Pallas kernels  30.5 us (97%)
  between operations  0.64 us (2%)
    pallas_call x1, Pallas kernels, body(): pl.pallas_call(functools.partial(kernel, nrow, ncol), out_shape=jax.Shape...  29.8 us
    pallas_call x1, Pallas kernels, body(): pl.pallas_call(hand_over, out_shape=[jax.ShapeDtypeStruct(surface.shape,...  0.7 us

profile of v7, /device:TPU:1, one launch (start us, length us, event | category | flops | bytes accessed | tf_op | source)
XLA Modules:
  0.0 31.1 jit_solution(4318468171724625432)
XLA Ops:
  0.6 29.8 %shard_map.85.fields = f32[3,2,64,128]{3,2,1,0:T(8,128)S(1)} custom-call(f32[2,64,128]{2,1,0:T(8,128)} %surf_h.1, f32[2,64,128]{2,1,0:T(8,128)} %u_h.1, f32[2,64,128]{2,1,0:T(8,128)} %v_h.1, f32[64,128]{1,0:T(8,128)} %bed_h.1, s32[2,64,128]{2,1,0:T(8,128)} %wet_h.1, f32[2,64,128]{2,1,0:T(8,128)} %rain_h.1), custom_call_target="tpu_custom_call" | custom-call | tf_op jit(solution)/shard_map/pallas_call | solution.py:429
  30.4 0.7 %shard_map.86 = (f32[2,64,128]{2,1,0:T(8,128)}, f32[2,64,128]{2,1,0:T(8,128)}, f32[2,64,128]{2,1,0:T(8,128)}) custom-call(f32[3,2,64,128]{3,2,1,0:T(8,128)S(1)} %shard_map.85.fields), custom_call_target="tpu_custom_call" | custom-call | tf_op jit(solution)/shard_map/pallas_call | solution.py:455
